TPU v7x, 256 devices: a whole 4x4x8 slice. The times are simulated.
256 devices in a mesh: rows: 32 (over y, x, core), cols: 8 (over z).
Axes of the slice: x: 4, y: 4, z: 8, core: 2. Of those that a mesh axis runs over, the one named last changes fastest.
Arguments:
- owner_map: int32 [2, 512], replicated, may hold values from 0 to 511, as said below
- colidx: int32 [2, 512, 24], P(None, 'rows', 'cols'), may hold values from 0 to 767, as said below
- live: int32 [2, 512], P(None, 'rows'), may hold values from 1 to 24
- blocks: bfloat16 [2, 512, 24, 128, 128], P(None, 'rows', 'cols'), may hold values from -0.15625 to 0.15625
- diag_inverse: float32 [2, 512, 128, 128], P(None, 'rows')
- right_side: float32 [2, 512, 64, 128], P(None, 'rows'), may hold values from -6 to 6
- prior: bfloat16 [256, 64, 128], P('rows'), may hold values from -6 to 6
Outputs:
- solved: float32 [2, 512, 64, 128], P(None, 'rows')
Inputs may be any that keep to these rules, and one draw needn't show every extreme that they name: Each row of owner_map is a permutation of the block rows of a front. `colidx`: front 0 refers only to earlier block rows; in front 1, even slots refer to rows of front 0 and odd slots to earlier block rows. Take the even slots of front 1 that lie in block rows s with s // 16 equal to one value and in slots j with j // 3 equal to one value. Among them, at most 1 refer to front-0 rows r whose slot t (owner_map[0, t] = r) has t // 16 equal to any single value; some such group reaches 1.
All inputs are finite; a program needn't handle non-finite values.
Results may differ from a plain program's by a relative error of at most 0.0017.
Values may be sent and summed in bfloat16 or wider, within the bound.
A program may use at most 64 MiB of HBM per device.

v0:
```python
import jax
import jax.numpy as jnp
from jax import lax
from jax.sharding import PartitionSpec as P


def solve_diag(resid, inverse):
    return jnp.einsum(
        "rpb,rcb->rpc",
        resid,
        inverse,
        precision=lax.Precision.HIGHEST,
        preferred_element_type=jnp.float32,
    )


def block_products(blk, values):
    return jnp.einsum("rjcb,rjpb->rpc", blk, values, preferred_element_type=jnp.float32)


def finish(partial_value, rhs_front, inverse):
    total = lax.psum(partial_value, "cols")
    return solve_diag(rhs_front - total, inverse)


def shards(owner_map, colidx, live, blocks, diag_inverse, right_side, prior):
    slot_count = blocks.shape[2]
    col_here = lax.axis_index("cols")
    rows_front = owner_map.shape[1]
    slot_ids = col_here * slot_count + jnp.arange(slot_count, dtype=jnp.int32)
    live_mask = slot_ids[None, None, :] < live[:, :, None]
    prior_all = lax.all_gather(prior, "rows", axis=0, tiled=True)
    prior_count = prior_all.shape[0]
    zero_value = jnp.zeros((), jnp.bfloat16)
    first_idx = jnp.clip(colidx[0], 0, prior_count - 1)
    first_values = jnp.where(live_mask[0][:, :, None, None], prior_all[first_idx], zero_value)
    first = finish(block_products(blocks[0], first_values), right_side[0], diag_inverse[0])
    first_low = first.astype(jnp.bfloat16)
    second_idx = colidx[1]
    from_prior = second_idx < prior_count
    inverse_map = (
        jnp.zeros((rows_front,), jnp.int32)
        .at[owner_map[0]]
        .set(jnp.arange(rows_front, dtype=jnp.int32))
    )
    slot_pos = inverse_map[jnp.clip(second_idx - prior_count, 0, rows_front - 1)]
    whole_front = lax.all_gather(first_low, "rows", axis=0, tiled=True)
    recent_values = whole_front[slot_pos]
    early_values = prior_all[jnp.clip(second_idx, 0, prior_count - 1)]
    chosen = jnp.where(from_prior[:, :, None, None], early_values, recent_values)
    second_values = jnp.where(live_mask[1][:, :, None, None], chosen, zero_value)
    second = finish(block_products(blocks[1], second_values), right_side[1], diag_inverse[1])
    return jnp.stack([first, second])


def solution(mesh):
    placed = (
        P(),
        P(None, "rows", "cols"),
        P(None, "rows"),
        P(None, "rows", "cols", None, None),
        P(None, "rows", None, None),
        P(None, "rows", None, None),
        P("rows", None, None),
    )
    return jax.shard_map(
        shards, mesh=mesh, in_specs=placed, out_specs=P(None, "rows", None, None), check_vma=False
    )
```

profile of v0, /device:TPU:1, one launch (start us, length us, event | category | flops | bytes accessed | tf_op | source)
XLA Modules:
  0.0 292.1 jit_solution(2289434202157852496)
XLA Ops:
  6.5 0.7 all-gather.3.cloned.1.call-update
  7.3 0.8 compare_select_fusion.2
  8.1 0.1 copy.29
  8.2 0.1 reshape.128
  8.3 0.8 broadcast_compare_fusion
  9.0 0.1 copy.28
  9.1 56.1 %all-gather.3.cloned.1.call-done = bf16[256,64,128]{2,1,0:T(8,128)(2,1)} async-done(((bf16[8,64,128]{2,1,0:T(8,128)(2,1)}), bf16[256,64,128]{2,1,0:T(8,128)(2,1)}) %all-gather.3.cloned.1.call-update) | async-done | bytes 4194320 | tf_op jit(solution)/shard_map/all_gather | solution.py:32
  65.2 2.9 gather_fusion
  68.2 3.0 %fusion.6 = f32[16,64,128]{2,1,0:T(8,128)} fusion(bf16[2,16,3,128,128]{4,3,2,1,0:T(8,128)(2,1)} %param.10, bf16[16,3,64,128]{3,2,1,0:T(8,128)(2,1)S(1)} %bitcast.63, pred[16,3]{1,0:T(8,128)(4,1)S(1)} %copy.28), kind=kOutput, calls=%fused_computation.11 | convolution fusion | flops 101056512 | bytes 2883632 | tf_op jit(solution)/shard_map/rjcb,rjpb->rpc/dot_general | solution.py:18
  71.2 0.0 all-gather.5.cloned.1.call-start
  71.3 68.0 %all-reduce.3.cloned.1.call-done = f32[16,64,128]{2,1,0:T(8,128)} async-done(((f32[16,64,128]{2,1,0:T(8,128)}), f32[16,64,128]{2,1,0:T(8,128)}) %all-reduce.3.cloned.1.call-update) | async-done | bytes 524304 | tf_op jit(solution)/shard_map/psum | solution.py:22
  139.2 4.0 %fusion.31 = (bf16[16,64,128]{2,1,0:T(8,128)(2,1)}, f32[16,64,128]{2,1,0:T(8,128)S(1)}) fusion(f32[2,16,128,128]{3,2,1,0:T(8,128)S(1)} %copy-done, f32[16,64,128]{2,1,0:T(8,128)} %all-reduce.3.cloned.1.call-done, f32[2,16,64,128]{3,2,1,0:T(8,128)} %param.12), kind=kOutput, calls=%fused_computation.50 | convolution fusion | flops 201588736 | bytes 2883584 | tf_op jit(solution)/shard_map/rpb,rcb->rpc/dot_general | solution.py:8
  143.3 0.0 all-reduce.5.cloned.1.call-start
  143.3 0.1 copy.32
  143.4 0.1 reshape.136
  143.5 0.1 copy.33
  143.6 0.1 reshape.144
  143.7 2.4 scatter_custom_fusion
  146.2 0.8 gather_fusion.2
  147.0 0.1 gather.17
  147.1 0.1 copy.34
  147.2 0.1 copy.37
  147.2 0.1 reshape.152
  147.4 0.1 copy.40
  147.5 0.1 copy.30
  147.6 2.9 gather_fusion.1
  150.5 54.3 %all-gather.5.cloned.1.call-done = bf16[512,64,128]{2,1,0:T(8,128)(2,1)} async-done(((bf16[16,64,128]{2,1,0:T(8,128)(2,1)}), bf16[512,64,128]{2,1,0:T(8,128)(2,1)}) %all-gather.5.cloned.1.call-update) | async-done | bytes 8388624 | tf_op jit(solution)/shard_map/all_gather | solution.py:47
  204.7 4.9 %gather_fusion.3 = bf16[48,64,128]{2,1,0:T(8,128)(2,1)} fusion(bf16[512,64,128]{2,1,0:T(8,128)(2,1)} %all-gather.5.cloned.1.call-done, s32[1024]{0:T(1024)S(1)} %pad_clamp_fusion), kind=kCustom, calls=%fused_computation.3 | custom fusion | bytes 1573056 | tf_op jit(solution)/shard_map/gather | solution.py:48
  209.7 3.3 %fusion.9 = f32[16,64,128]{2,1,0:T(8,128)} fusion(bf16[2,16,3,128,128]{4,3,2,1,0:T(8,128)(2,1)} %param.10, bf16[16,3,64,128]{3,2,1,0:T(8,128)(2,1)S(1)} %bitcast.61, bf16[16,3,64,128]{3,2,1,0:T(8,128)(2,1)} %bitcast.62, pred[16,3]{1,0:T(8,128)(4,1)S(1)} %bitcast.64, pred[16,3]{1,0:T(8,128)(4,1)S(1)} %copy.30), kind=kOutput, calls=%fused_computation.12 | convolution fusion | flops 101449728 | bytes 3670112 | tf_op jit(solution)/shard_map/rjcb,rjpb->rpc/dot_general | solution.py:18
  213.0 68.2 %all-reduce.5.cloned.1.call-done = f32[16,64,128]{2,1,0:T(8,128)} async-done(((f32[16,64,128]{2,1,0:T(8,128)}), f32[16,64,128]{2,1,0:T(8,128)}) %all-reduce.5.cloned.1.call-update) | async-done | bytes 524304 | tf_op jit(solution)/shard_map/psum | solution.py:22
  281.2 3.3 %convolution_bitcast_fusion = f32[1,16,64,128]{3,2,1,0:T(8,128)S(1)} fusion(f32[2,16,128,128]{3,2,1,0:T(8,128)S(1)} %copy-done, f32[16,64,128]{2,1,0:T(8,128)} %all-reduce.5.cloned.1.call-done, f32[2,16,64,128]{3,2,1,0:T(8,128)} %param.12), kind=kOutput, calls=%fused_computation.13 | convolution fusion | flops 201457664 | bytes 2621440 | tf_op jit(solution)/shard_map/rpb,rcb->rpc/dot_general | solution.py:8
  284.5 1.1 pad_maximum_fusion
  (21 shorter events, 0.2 us)
Async XLA Ops:
  6.5 132.7 %copy-start = (f32[2,16,128,128]{3,2,1,0:T(8,128)S(1)}, f32[2,16,128,128]{3,2,1,0:T(8,128)}, u32[]{:S(2)}) copy-start(f32[2,16,128,128]{3,2,1,0:T(8,128)} %param.11) | copy-start | bytes 6291460
  6.5 58.7 %all-gather.3.cloned.1.call-start = ((), (), s32[]{:S(2)}) async-start(), calls=%async_computation | async-start | bytes 4325376 | tf_op jit(solution)/shard_map/all_gather | solution.py:32
  7.3 132.0 %all-reduce.3.cloned.1.call-start = ((), (), s32[]{:S(2)}) async-start(), calls=%async_computation.1 | async-start | bytes 1048576 | tf_op jit(solution)/shard_map/psum | solution.py:22
  68.1 75.6 %copy-start.2 = (s32[2,512]{1,0:T(2,128)S(1)}, s32[2,512]{1,0:T(2,128)}, u32[]{:S(2)}) copy-start(s32[2,512]{1,0:T(2,128)} %param.7) | copy-start | bytes 12292
  71.2 133.5 %all-gather.5.cloned.1.call-start = ((), (), s32[]{:S(2)}) async-start(), calls=%async_computation.2 | async-start | bytes 8650752 | tf_op jit(solution)/shard_map/all_gather | solution.py:47
  143.3 137.9 %all-reduce.5.cloned.1.call-start = ((), (), s32[]{:S(2)}) async-start(), calls=%async_computation.3 | async-start | bytes 1048576 | tf_op jit(solution)/shard_map/psum | solution.py:22
  146.2 1.2 copy-start.1
Sparse Core Ops, SparseCore 0:
  9.9 55.2 all-gather.2
  71.3 67.8 all-reduce.2
  143.4 61.2 all-gather.4
  213.1 68.0 all-reduce.4
where the time goes:
time: 296 us; the launch traced here: 292 us
  waiting for transfers between devices  247 us (83%)
  local copies, waits for them, and re-layouts  15.1 us (5%)
  matrix products  13.7 us (5%)
  between operations  13.3 us (4%)
    psum x2, waiting for transfers between devices, finish(): total = lax.psum(partial_value, 'cols')  136 us
    all_gather x1, waiting for transfers between devices, shards(): prior_all = lax.all_gather(prior, 'rows', axis=0, tiled=True)  56.1 us
    all_gather x1, waiting for transfers between devices, shards(): whole_front = lax.all_gather(first_low, 'rows', axis=0, tiled=True)  54.3 us
    dot_general x2, matrix products, solve_diag(): jnp.einsum('rpb,rcb->rpc', resid, inverse, precision=lax.Precision.HIGHES...  7.34 us
    dot_general x2, matrix products, block_products(): jnp.einsum('rjcb,rjpb->rpc', blk, values, preferred_element_type=jnp.floa...  6.37 us
  transfers between devices with their start and end apart: 4, of which 4 were waited for; matrix products, arithmetic and copies ran while one was open for 3% of the time, Pallas kernels for 0%

commit v1 on v0

v1 whole, which is shorter than its diff:
```python
import functools

import jax
import jax.numpy as jnp
from jax import lax
from jax.experimental import pallas as pl
from jax.experimental.pallas import tpu as pltpu
from jax.sharding import PartitionSpec as P

MESH = pl.DeviceIdType.MESH
NX, NY, NCORE, NZ = 4, 4, 2, 8
NR = NX * NY * NCORE
PRI_DEV = 8
NPRI = NR * PRI_DEV
ROWS_DEV = 16
SEG = ROWS_DEV // NZ
NBC = 3
P_SIZE, B = 64, 128
NT = (((1,), (1,)), ((), ()))
ORDER = (4, 3, 5, 2, 6, 1, 7, 0)


def kernel(
    tbl, want, blocks, dinv, rhs, prior, out,
    known, recent, blk, dv, rh, part, rs, sol, low, a2a, want_in, sel,
    loc_sem, out_sem, w_s, w_r, t_s, t_r, sib_s, sib_r, rs_s, rs_r, ag_s, ag_r, a_s, a_r,
):
    r = lax.axis_index("rows")
    c = lax.axis_index("cols")
    core = lax.rem(r, 2)
    cx = lax.rem(r // 2, NX)
    cy = r // (2 * NX)

    def rid(y, x, k):
        return (lax.rem(y + NY, NY) * NX + lax.rem(x + NX, NX)) * 2 + k

    def remote(src, dst, ss, rr, dev):
        return pltpu.make_async_remote_copy(
            src_ref=src, dst_ref=dst, send_sem=ss, recv_sem=rr, device_id=dev, device_id_type=MESH
        )

    own = known.at[pl.ds(r * PRI_DEV, PRI_DEV)]
    ld_prior = pltpu.make_async_copy(prior, own, loc_sem.at[0])
    ld_blk = pltpu.make_async_copy(blocks, blk, loc_sem.at[1])
    ld_dv = pltpu.make_async_copy(dinv.at[:, pl.ds(c * SEG, SEG)], dv, loc_sem.at[2])
    ld_rh = pltpu.make_async_copy(rhs.at[:, pl.ds(c * SEG, SEG)], rh, loc_sem.at[3])
    ld_prior.start()
    ld_blk.start()
    ld_dv.start()
    ld_rh.start()
    known[NPRI] = jnp.zeros((P_SIZE, B), jnp.bfloat16)
    recent[NR] = jnp.zeros((P_SIZE, B), jnp.bfloat16)

    barrier = pltpu.get_barrier_semaphore()

    def greet_rows(e, carry):
        pl.semaphore_signal(barrier, inc=1, device_id=(lax.rem(r + e, NR), c), device_id_type=MESH)
        return carry

    def greet_cols(e, carry):
        pl.semaphore_signal(barrier, inc=1, device_id=(r, lax.rem(c + e, NZ)), device_id_type=MESH)
        return carry

    lax.fori_loop(1, NR, greet_rows, 0)
    lax.fori_loop(1, NZ, greet_cols, 0)
    pl.semaphore_wait(barrier, NR - 1 + NZ - 1)
    ld_prior.wait()

    sends = []

    def src_rows(h, du, dv_, lo, n):
        x, y = (cx - du, cy - dv_) if h == 0 else (cx - dv_, cy - du)
        base = rid(y + NY, x + NX, core) * PRI_DEV + h * 4 + lo
        return known.at[pl.ds(base, n)]

    def neighbour(h, du, dv_):
        x, y = (cx + du, cy + dv_) if h == 0 else (cx + dv_, cy + du)
        return (rid(y + NY, x + NX, core), c)

    sem_of = {}

    def recv_id(h, du, dv_, q):
        return h * 32 + ((du + 4) % 4) * 8 + ((dv_ + 4) % 4) * 2 + q

    def push(h, item, step, lo, n, q):
        rows = src_rows(h, item[0], item[1], lo, n)
        got = recv_id(h, item[0] + step[0], item[1] + step[1], q)
        i = len(sends)
        cp = remote(rows, rows, t_s.at[i], t_r.at[got], neighbour(h, *step))
        cp.start()
        sends.append(cp)

    def arrive(h, item, lo, n, q):
        rows = src_rows(h, item[0], item[1], lo, n)
        got = recv_id(h, item[0], item[1], q)
        remote(rows, rows, t_s.at[0], t_r.at[got], (r, c)).wait_recv()

    sib = []

    def to_sibling(h, item):
        rows = src_rows(h, item[0], item[1], 0, 4)
        i = len(sib)
        j = h * 16 + ((item[0] + 4) % 4) * 4 + ((item[1] + 4) % 4)
        cp = remote(rows, rows, sib_s.at[i], sib_r.at[j], (rid(cy + NY, cx + NX, 1 - core), c))
        cp.start()
        sib.append((cp, h, item, j))

    def spread(h, item):
        push(h, item, (0, 1), 0, 4, 0)
        push(h, item, (0, -1), 0, 4, 0)

    for h in (0, 1):
        push(h, (0, 0), (1, 0), 0, 4, 0)
        push(h, (0, 0), (-1, 0), 0, 4, 0)
    for h in (0, 1):
        spread(h, (0, 0))
        to_sibling(h, (0, 0))
    for h in (0, 1):
        arrive(h, (1, 0), 0, 4, 0)
        push(h, (1, 0), (1, 0), 0, 2, 0)
        arrive(h, (-1, 0), 0, 4, 0)
        push(h, (-1, 0), (-1, 0), 2, 2, 1)
        for du in (1, -1):
            spread(h, (du, 0))
            to_sibling(h, (du, 0))

    def ask(e, carry):
        peer = lax.rem(r + e, NR)
        remote(want.at[peer], want_in.at[r], w_s.at[e], w_r.at[e], (peer, c)).start()
        return carry

    lax.fori_loop(1, NR, ask, 0)
    keep_own = pltpu.make_async_copy(want.at[r], want_in.at[r], loc_sem.at[4])
    keep_own.start()

    def second(h, du):
        arrive(h, (du, 1), 0, 4, 0)
        push(h, (du, 1), (0, 1), 0, 2, 0)
        to_sibling(h, (du, 1))
        arrive(h, (du, -1), 0, 4, 0)
        push(h, (du, -1), (0, -1), 2, 2, 1)
        to_sibling(h, (du, -1))

    def far(h, du, dv_):
        if du == 2 and dv_ == 0:
            arrive(h, (2, 0), 0, 2, 0)
            arrive(h, (2, 0), 2, 2, 1)
        else:
            arrive(h, (du, 2), 0, 2, 0)
            arrive(h, (du, 2), 2, 2, 1)
        to_sibling(h, (du, dv_))

    for h in (0, 1):
        second(h, 0)
    for h in (0, 1):
        far(h, 2, 0)
        spread(h, (2, 0))
    for du in (1, -1):
        for h in (0, 1):
            second(h, du)
    for h in (0, 1):
        far(h, 0, 2)
    for h in (0, 1):
        second(h, 2)
    for du in (1, -1, 2):
        for h in (0, 1):
            far(h, du, 2)
    for cp, h, item, j in sib:
        x, y = (cx - item[0], cy - item[1]) if h == 0 else (cx - item[1], cy - item[0])
        base = rid(y + NY, x + NX, 1 - core) * PRI_DEV + h * 4
        rows = known.at[pl.ds(base, 4)]
        remote(rows, rows, sib_s.at[0], sib_r.at[j], (r, c)).wait_recv()
    ld_blk.wait()

    def product(f, s, held, slots):
        xs = jnp.concatenate([held[tbl[f, s * NBC + j]] for j in slots], axis=1)
        ws = jnp.concatenate([blk[f, s, j] for j in slots], axis=1)
        return lax.dot_general(xs, ws, NT, preferred_element_type=jnp.float32)

    def rows_of(peer, body):
        def one(q, carry):
            body(peer * SEG + q)
            return carry

        lax.fori_loop(0, SEG, one, 0)

    def scatter(f, d, peer):
        remote(
            part.at[f, pl.ds(peer * SEG, SEG)], rs.at[f, d], rs_s.at[f, d], rs_r.at[f, d], (r, peer)
        ).start()

    def first_products():
        for d in ORDER:
            peer = lax.rem(c + d, NZ)

            def body(s):
                part[0, s] = product(0, s, known, (0, 1, 2))

            rows_of(peer, body)
            if d != 0:
                scatter(0, d, peer)

    even_col = lax.rem(c, 2) == 0

    def early_products():
        def step(slots):
            def one(s, carry):
                part[1, s] = product(1, s, known, slots)
                return carry

            lax.fori_loop(0, ROWS_DEV, one, 0)

        pl.when(even_col)(lambda: step((1,)))
        pl.when(jnp.logical_not(even_col))(lambda: step((0, 2)))

    def late_products():
        for d in ORDER:
            peer = lax.rem(c + d, NZ)

            def step(slots):
                def body(s):
                    part[1, s] += product(1, s, recent, slots)

                rows_of(peer, body)

            pl.when(even_col)(lambda: step((0, 2)))
            pl.when(jnp.logical_not(even_col))(lambda: step((1,)))
            if d != 0:
                scatter(1, d, peer)

    def finish(f):
        for d in range(1, NZ):
            remote(
                part.at[f, pl.ds(0, SEG)], rs.at[f, d], rs_s.at[f, d], rs_r.at[f, d], (r, lax.rem(c + d, NZ))
            ).wait_recv()
        for q in range(SEG):
            total = part[f, c * SEG + q]
            for d in range(1, NZ):
                total = total + rs[f, d, q]
            sol[f, c * SEG + q] = lax.dot_general(
                rh[f, q] - total, dv[f, q], NT,
                precision=lax.Precision.HIGHEST, preferred_element_type=jnp.float32,
            )
        mine = sol.at[f, pl.ds(c * SEG, SEG)]
        for d in ORDER[:-1]:
            peer = lax.rem(c + d, NZ)
            remote(mine, mine, ag_s.at[f, d], ag_r.at[f, d], (r, peer)).start()
        for d in ORDER[:-1]:
            theirs = sol.at[f, pl.ds(lax.rem(c + NZ - d, NZ) * SEG, SEG)]
            remote(theirs, theirs, ag_s.at[f, d], ag_r.at[f, d], (r, c)).wait_recv()

    first_products()
    early_products()
    ld_dv.wait()
    ld_rh.wait()
    finish(0)

    def asked(e, carry):
        remote(want.at[0], want_in.at[lax.rem(r + NR - e, NR)], w_s.at[e], w_r.at[e], (r, c)).wait_recv()
        return carry

    lax.fori_loop(1, NR, asked, 0)
    keep_own.wait()
    to_scalar = pltpu.make_async_copy(want_in, sel, loc_sem.at[5])
    to_scalar.start()
    out0 = pltpu.make_async_copy(sol.at[0], out.at[0], out_sem.at[0])
    out0.start()

    def narrow(i, carry):
        low[i] = sol[0, i].astype(jnp.bfloat16)
        return carry

    lax.fori_loop(0, ROWS_DEV, narrow, 0)
    to_scalar.wait()

    def give(e, carry):
        peer = lax.rem(r + e, NR)
        a2a[e] = low[sel[peer, 0, 0]]
        remote(a2a.at[e], recent.at[r], a_s.at[e], a_r.at[e], (peer, c)).start()
        return carry

    lax.fori_loop(1, NR, give, 0)
    recent[r] = low[sel[r, 0, 0]]

    def take(e, carry):
        slot = recent.at[lax.rem(r + NR - e, NR)]
        remote(slot, slot, a_s.at[e], a_r.at[e], (r, c)).wait_recv()
        return carry

    lax.fori_loop(1, NR, take, 0)

    late_products()
    finish(1)
    out1 = pltpu.make_async_copy(sol.at[1], out.at[1], out_sem.at[1])
    out1.start()

    for cp in sends:
        cp.wait_send()
    for cp, h, item, j in sib:
        cp.wait_send()

    def left(e, carry):
        peer = lax.rem(r + e, NR)
        remote(want.at[peer], want_in.at[r], w_s.at[e], w_r.at[e], (peer, c)).wait_send()
        remote(a2a.at[e], recent.at[r], a_s.at[e], a_r.at[e], (peer, c)).wait_send()
        return carry

    lax.fori_loop(1, NR, left, 0)
    for f in (0, 1):
        mine = sol.at[f, pl.ds(c * SEG, SEG)]
        for d in range(1, NZ):
            peer = lax.rem(c + d, NZ)
            remote(
                part.at[f, pl.ds(peer * SEG, SEG)], rs.at[f, d], rs_s.at[f, d], rs_r.at[f, d], (r, peer)
            ).wait_send()
            remote(mine, mine, ag_s.at[f, d], ag_r.at[f, d], (r, peer)).wait_send()
    out0.wait()
    out1.wait()


def shards(owner_map, colidx, live, blocks, diag_inverse, right_side, prior):
    col_here = lax.axis_index("cols")
    slot_ids = col_here * NBC + jnp.arange(NBC, dtype=jnp.int32)
    live_mask = slot_ids[None, None, :] < live[:, :, None]
    rows_front = owner_map.shape[1]
    row = colidx[1].reshape(-1) - NPRI
    slots = jnp.arange(rows_front, dtype=jnp.int32)
    place = jnp.sum(jnp.where(row[:, None] == owner_map[0][None, :], slots[None, :], 0), axis=1)
    recent = row >= 0
    holder = jnp.where(recent, place // ROWS_DEV, -1)
    second = jnp.where(recent, holder, row + NPRI).reshape(ROWS_DEV, NBC)
    both = jnp.stack([colidx[0], second])
    empty = jnp.stack([jnp.full((ROWS_DEV * NBC,), NPRI), jnp.where(recent, NR, NPRI)]).reshape(2, ROWS_DEV, NBC)
    tbl = jnp.where(live_mask, both, empty).reshape(2, ROWS_DEV * NBC)
    want = jnp.max(
        jnp.where(jnp.arange(NR, dtype=jnp.int32)[:, None] == holder[None, :], (place % ROWS_DEV)[None, :], 0), axis=1
    )
    want = jnp.broadcast_to(want[:, None, None], (NR, 1, B))
    dma = pltpu.SemaphoreType.DMA
    any_spec = pl.BlockSpec(memory_space=pl.ANY)
    return pl.pallas_call(
        kernel,
        out_shape=jax.ShapeDtypeStruct((2, ROWS_DEV, P_SIZE, B), jnp.float32),
        in_specs=[
            pl.BlockSpec(memory_space=pltpu.SMEM),
            pl.BlockSpec(memory_space=pltpu.VMEM),
            any_spec, any_spec, any_spec, any_spec,
        ],
        out_specs=any_spec,
        scratch_shapes=[
            pltpu.VMEM((NPRI + 1, P_SIZE, B), jnp.bfloat16),
            pltpu.VMEM((NR + 1, P_SIZE, B), jnp.bfloat16),
            pltpu.VMEM((2, ROWS_DEV, NBC, B, B), jnp.bfloat16),
            pltpu.VMEM((2, SEG, B, B), jnp.float32),
            pltpu.VMEM((2, SEG, P_SIZE, B), jnp.float32),
            pltpu.VMEM((2, ROWS_DEV, P_SIZE, B), jnp.float32),
            pltpu.VMEM((2, NZ, SEG, P_SIZE, B), jnp.float32),
            pltpu.VMEM((2, ROWS_DEV, P_SIZE, B), jnp.float32),
            pltpu.VMEM((ROWS_DEV, P_SIZE, B), jnp.bfloat16),
            pltpu.VMEM((NR, P_SIZE, B), jnp.bfloat16),
            pltpu.VMEM((NR, 1, B), jnp.int32),
            pltpu.SMEM((NR, 1, B), jnp.int32),
            dma((6,)), dma((2,)),
            dma((NR,)), dma((NR,)),
            dma((40,)), dma((64,)),
            dma((32,)), dma((32,)),
            dma((2, NZ)), dma((2, NZ)),
            dma((2, NZ)), dma((2, NZ)),
            dma((NR,)), dma((NR,)),
        ],
        compiler_params=pltpu.CompilerParams(
            collective_id=0, has_side_effects=True, vmem_limit_bytes=40 * 1024 * 1024
        ),
    )(tbl, want, blocks, diag_inverse, right_side, prior)


def solution(mesh):
    placed = (
        P(),
        P(None, "rows", "cols"),
        P(None, "rows"),
        P(None, "rows", "cols", None, None),
        P(None, "rows", None, None),
        P(None, "rows", None, None),
        P("rows", None, None),
    )
    return jax.shard_map(
        shards, mesh=mesh, in_specs=placed, out_specs=P(None, "rows", None, None), check_vma=False
    )
```

time: 296 us -> 110 us (0.37); the launches traced: 292 us -> 109 us
  waiting for transfers between devices: 247 us -> 0 us
  Pallas kernels: 0 us -> 99.2 us
  matrix products: 13.7 us -> 0 us
  between operations: 13.3 us -> 0.08 us
  local copies, waits for them, and re-layouts: 15.1 us -> 9.64 us
    psum x2 -> x0, waiting for transfers between devices: 136 us -> none  [finish(): total = lax.psum(partial_value, 'cols')]
    all_gather x2 -> x0, waiting for transfers between devices: 110 us -> none  [the longest x1 56.1 us: shards(): prior_all = lax.all_gather(prior, 'rows', axis=0, tiled=True)]
    pallas_call x0 -> x1, Pallas kernels: none -> 99.2 us  [shards(): pl.pallas_call(kernel, out_shape=jax.ShapeDtypeStruct((2, ROWS_DEV, P_SIZ...]
    dot_general x4 -> x0, matrix products: 13.7 us -> none  [the longest x2 7.34 us: solve_diag(): jnp.einsum('rpb,rcb->rpc', resid, inverse, precision=lax.Precision.HIGHES...]
    gather x6 -> x0, local copies, waits for them, and re-layouts: 11.7 us -> none  [the longest x1 4.93 us: shards(): recent_values = whole_front[slot_pos]]
    unnamed x6 -> x10, local copies, waits for them, and re-layouts: 0.02 us -> 6.66 us
  transfers between devices with their start and end apart: 4 -> 0, of which waited for: 4 -> 0; matrix products, arithmetic and copies ran while one was open for 3% -> 0% of each run, Pallas kernels for 0% -> 0%
where the time goes in v1:
time: 110 us; the launch traced here: 109 us
  Pallas kernels  99.2 us (90%)
  local copies, waits for them, and re-layouts  9.64 us (9%)
    pallas_call x1, Pallas kernels, shards(): pl.pallas_call(kernel, out_shape=jax.ShapeDtypeStruct((2, ROWS_DEV, P_SIZ...  99.2 us
    unnamed x10, local copies, waits for them, and re-layouts  6.66 us

profile of v1, /device:TPU:1, one launch (start us, length us, event | category | flops | bytes accessed | tf_op | source)
XLA Modules:
  0.0 109.2 jit_solution(12717783565423904073)
XLA Ops:
  0.0 0.7 slice.11
  0.7 0.8 fusion.2
  1.5 0.1 copy.12
  1.5 0.1 stack.11
  1.6 0.1 lt.27
  1.7 0.1 copy.14
  1.8 0.1 sub.14
  1.9 0.2 select_reduce_fusion
  2.1 0.1 select_reduce_fusion.1
  2.2 0.1 reduce_sum.12
  2.3 0.1 select_n.76
  2.4 0.1 stack.12
  2.5 0.1 broadcast_in_dim.50.want
  2.6 0.8 lt.29
  3.4 0.1 lt.30
  3.5 0.0 copy-start
  3.5 1.9 %copy-done = bf16[2,16,3,128,128]{4,3,2,1,0:T(8,128)(2,1)S(1)} copy-done((bf16[2,16,3,128,128]{4,3,2,1,0:T(8,128)(2,1)S(1)}, bf16[2,16,3,128,128]{4,3,2,1,0:T(8,128)(2,1)}, u32[]{:S(2)}) %copy-start) | copy-done | bytes 3145752
  5.4 0.0 copy-start.1
  5.4 1.6 %copy-done.1 = f32[2,16,128,128]{3,2,1,0:T(8,128)S(1)} copy-done((f32[2,16,128,128]{3,2,1,0:T(8,128)S(1)}, f32[2,16,128,128]{3,2,1,0:T(8,128)}, u32[]{:S(2)}) %copy-start.1) | copy-done | bytes 2097176
  7.0 0.0 copy-start.2
  7.0 1.2 %copy-done.2 = f32[2,16,64,128]{3,2,1,0:T(8,128)S(1)} copy-done((f32[2,16,64,128]{3,2,1,0:T(8,128)S(1)}, f32[2,16,64,128]{3,2,1,0:T(8,128)}, u32[]{:S(2)}) %copy-start.2) | copy-done | bytes 1048600
  8.2 0.0 copy-start.3
  8.2 0.9 copy-done.3
  9.1 99.2 %shard_map.73 = f32[2,16,64,128]{3,2,1,0:T(8,128)S(1)} custom-call(s32[2,48]{1,0:T(2,128)S(1)} %compare_select_fusion.1.tbl, s32[32,1,128]{2,1,0:T(1,128)S(1)} %broadcast_in_dim.50.want, bf16[2,16,3,128,128]{4,3,2,1,0:T(8,128)(2,1)S(1)} %copy-done, f32[2,16,128,128]{3,2,1,0:T(8,128)S(1)} %copy-done.1, f32[2,16,64,128]{3,2,1,0:T(8,128)S(1)} %copy-done.2, ...), custom_call_target="tpu_custom_call" | custom-call | tf_op jit(solution)/shard_map/pallas_call | solution.py:341
  108.3 1.0 copy.16
  (6 shorter events, 0.1 us)
Async XLA Ops:
  3.5 1.9 %copy-start = (bf16[2,16,3,128,128]{4,3,2,1,0:T(8,128)(2,1)S(1)}, bf16[2,16,3,128,128]{4,3,2,1,0:T(8,128)(2,1)}, u32[]{:S(2)}) copy-start(bf16[2,16,3,128,128]{4,3,2,1,0:T(8,128)(2,1)} %blocks.1) | copy-start | bytes 9437188
  5.4 1.6 %copy-start.1 = (f32[2,16,128,128]{3,2,1,0:T(8,128)S(1)}, f32[2,16,128,128]{3,2,1,0:T(8,128)}, u32[]{:S(2)}) copy-start(f32[2,16,128,128]{3,2,1,0:T(8,128)} %dinv.1) | copy-start | bytes 6291460
  7.0 1.2 %copy-start.2 = (f32[2,16,64,128]{3,2,1,0:T(8,128)S(1)}, f32[2,16,64,128]{3,2,1,0:T(8,128)}, u32[]{:S(2)}) copy-start(f32[2,16,64,128]{3,2,1,0:T(8,128)} %rhs.1) | copy-start | bytes 3145732
  8.2 0.9 copy-start.3

commit v2 on v0

v2 whole, which is shorter than its diff:
```python
import jax
import jax.numpy as jnp
from jax import lax
from jax.experimental import pallas as pl
from jax.experimental.pallas import tpu as pltpu
from jax.sharding import PartitionSpec as P

MESH = pl.DeviceIdType.MESH
NX, NY, NZ = 4, 4, 8
NR = NX * NY * 2
PRI_DEV = 8
HALF = PRI_DEV // 2
NPRI = NR * PRI_DEV
ROWS_DEV = 16
ROWS_F = NR * ROWS_DEV
SEG = ROWS_DEV // NZ
NBC = 3
SLOTS = ROWS_DEV * NBC
P_SIZE, B = 64, 128
SEG_ROWS = SEG * P_SIZE
CODED = SEG_ROWS + 16
NT = (((1,), (1,)), ((), ()))
PEERS = (4, 3, 5, 2, 6, 1, 7)


def encode(value):
    top = jnp.maximum(jnp.max(jnp.abs(value), axis=0, keepdims=True), 1e-30)
    power = jnp.ceil(jnp.log2(top) + 0.01)
    fixed = jnp.round(value * jnp.exp2(15.0 - power)).astype(jnp.int32).astype(jnp.int16)
    powers = jnp.broadcast_to(power, (16, B)).astype(jnp.int32).astype(jnp.int16)
    return fixed, powers


def decode(fixed, powers):
    unit = jnp.exp2(powers.astype(jnp.int32).astype(jnp.float32) - 15.0)
    value = fixed.astype(jnp.int32).astype(jnp.float32).reshape(SEG_ROWS // 16, 16, B) * unit[None]
    return value.reshape(SEG_ROWS, B)


def kernel(
    owners, cols, live, blocks, dinv, rhs, prior, out,
    known, recent, blk, dv, rh, part, own, code_s, code_r, fin, low, rest, a2a,
    om, place, want, want_in, col_s, live_s, place_s, sel,
    loc_sem, w_s, w_r, t_s, t_r, sib_s, sib_r, rs_s, rs_r, hi_s, hi_r, lo_s, lo_r, fin_s, fin_r, a_s, a_r,
):
    r = lax.axis_index("rows")
    c = lax.axis_index("cols")
    core = lax.rem(r, 2)
    cx = lax.rem(r // 2, NX)
    cy = r // (2 * NX)

    def rid(y, x, k):
        return (lax.rem(y + 2 * NY, NY) * NX + lax.rem(x + 2 * NX, NX)) * 2 + k

    def remote(src, dst, ss, rr, dev):
        return pltpu.make_async_remote_copy(
            src_ref=src, dst_ref=dst, send_sem=ss, recv_sem=rr, device_id=dev, device_id_type=MESH
        )

    locals_ = [
        pltpu.make_async_copy(src, dst, loc_sem.at[i])
        for i, (src, dst) in enumerate((
            (prior, known.at[pl.ds(r * PRI_DEV, PRI_DEV)]),
            (cols, col_s),
            (owners, om),
            (live, live_s),
            (blocks, blk),
            (dinv.at[:, pl.ds(c * SEG, SEG)], dv),
            (rhs.at[:, pl.ds(c * SEG, SEG)], rh),
        ))
    ]
    for cp in locals_:
        cp.start()
    ld_prior, ld_cols, ld_owners, ld_live, ld_blk, ld_dv, ld_rh = locals_

    barrier = pltpu.get_barrier_semaphore()

    def greet_rows(e, carry):
        pl.semaphore_signal(barrier, inc=1, device_id=(lax.rem(r + e, NR), c), device_id_type=MESH)
        return carry

    def greet_cols(e, carry):
        pl.semaphore_signal(barrier, inc=1, device_id=(r, lax.rem(c + e, NZ)), device_id_type=MESH)
        return carry

    lax.fori_loop(1, NR, greet_rows, 0)
    lax.fori_loop(1, NZ, greet_cols, 0)

    known[NPRI] = jnp.zeros((P_SIZE, B), jnp.bfloat16)
    recent[NR] = jnp.zeros((P_SIZE, B), jnp.bfloat16)

    ld_cols.wait()
    ld_owners.wait()
    ld_live.wait()
    ids = om[0:1, :]
    spots = lax.broadcasted_iota(jnp.int32, (1, ROWS_F), 1)

    def find(s, carry):
        for j in range(NBC):
            row = col_s[j, 1, s] - NPRI
            at = jnp.sum(jnp.where(ids == row, spots + 1, 0), axis=1, keepdims=True)
            place[s * NBC + j] = jnp.broadcast_to(at - 1, (1, B))
        return carry

    lax.fori_loop(0, ROWS_DEV, find, 0)
    to_place = pltpu.make_async_copy(place, place_s, loc_sem.at[7])
    to_place.start()
    lanes = lax.broadcasted_iota(jnp.int32, (SLOTS, 1, B), 2)
    spot = place[...]
    want[...] = jnp.max(jnp.where((spot >> 4) == lanes, spot & 15, 0), axis=0)
    pl.semaphore_wait(barrier, NR - 1 + NZ - 1)
    ld_prior.wait()

    sends = []

    def xy(h, a, b):
        return (a, b) if h == 0 else (b, a)

    def src_rows(h, item, lo, n, k):
        dx, dy = xy(h, *item)
        return known.at[pl.ds(rid(cy - dy, cx - dx, k) * PRI_DEV + h * HALF + lo, n)]

    def recv_id(h, item, q):
        return h * 32 + ((item[0] + 4) % 4) * 8 + ((item[1] + 4) % 4) * 2 + q

    def push(h, item, step, lo=0, n=HALF, q=0):
        rows = src_rows(h, item, lo, n, core)
        dx, dy = xy(h, *step)
        got = recv_id(h, (item[0] + step[0], item[1] + step[1]), q)
        cp = remote(rows, rows, t_s.at[len(sends)], t_r.at[got], (rid(cy + dy, cx + dx, core), c))
        cp.start()
        sends.append(cp)

    def arrive(h, item, lo=0, n=HALF, q=0):
        rows = src_rows(h, item, lo, n, core)
        remote(rows, rows, t_s.at[0], t_r.at[recv_id(h, item, q)], (r, c)).wait_recv()

    sib = []

    def to_sibling(h, item):
        rows = src_rows(h, item, 0, HALF, core)
        i = len(sib)
        cp = remote(rows, rows, sib_s.at[i], sib_r.at[i], (rid(cy, cx, 1 - core), c))
        cp.start()
        sib.append((cp, h, item))

    def spread(h, item):
        push(h, item, (0, 1))
        push(h, item, (0, -1))

    for h in (0, 1):
        push(h, (0, 0), (1, 0))
        push(h, (0, 0), (-1, 0))
    for h in (0, 1):
        push(h, (0, 0), (2, 0))
        spread(h, (0, 0))
    for h in (0, 1):
        to_sibling(h, (0, 0))

    def ask(e, carry):
        peer = lax.rem(r + e, NR)
        remote(want, want_in.at[r], w_s.at[e], w_r.at[e], (peer, c)).start()
        return carry

    lax.fori_loop(1, NR, ask, 0)
    keep_own = pltpu.make_async_copy(want, want_in.at[r], loc_sem.at[8])
    keep_own.start()

    for du in (1, -1):
        for h in (0, 1):
            arrive(h, (du, 0))
            spread(h, (du, 0))
            to_sibling(h, (du, 0))

    def relay(h, du):
        for dv_, lo, q in ((1, 0, 0), (-1, HALF // 2, 1)):
            arrive(h, (du, dv_))
            push(h, (du, dv_), (0, dv_), lo, HALF // 2, q)
            to_sibling(h, (du, dv_))

    for h in (0, 1):
        arrive(h, (2, 0))
        spread(h, (2, 0))
        push(h, (2, 0), (0, 2))
        to_sibling(h, (2, 0))
    for du in (0, 1, -1):
        for h in (0, 1):
            relay(h, du)
    for du in (0, 1, -1):
        for h in (0, 1):
            for q in (0, 1):
                arrive(h, (du, 2), q * HALF // 2, HALF // 2, q)
            to_sibling(h, (du, 2))
    for dv_ in (1, -1, 2):
        for h in (0, 1):
            arrive(h, (2, dv_))
            to_sibling(h, (2, dv_))
    ld_blk.wait()
    for i, (cp, h, item) in enumerate(sib):
        rows = src_rows(h, item, 0, HALF, 1 - core)
        remote(rows, rows, sib_s.at[0], sib_r.at[i], (r, c)).wait_recv()

    def product(f, s, held, index, slots):
        xs = jnp.concatenate([held[index(s, j)] for j in slots], axis=1)
        ws = jnp.concatenate([blk[f, s, j] for j in slots], axis=1)
        return lax.dot_general(xs, ws, NT, preferred_element_type=jnp.float32)

    def old_index(f):
        return lambda s, j: jnp.where(c * NBC + j < live_s[f, s], col_s[j, f, s], NPRI)

    def new_index(s, j):
        return jnp.where(c * NBC + j < live_s[1, s], place_s[s * NBC + j, 0, 0] >> 4, NR)

    def code_copy(f, d):
        return remote(
            code_s.at[f, d], code_r.at[f, d], rs_s.at[f, d], rs_r.at[f, d], (r, lax.rem(c + d, NZ))
        )

    def put(ref, value):
        fixed, powers = encode(value)
        ref[0:SEG_ROWS] = fixed
        ref[SEG_ROWS:CODED] = powers

    def scatter(f, row):
        for d in PEERS:
            peer = lax.rem(c + d, NZ)
            put(code_s.at[f, d], jnp.concatenate([row(peer * SEG + q) for q in range(SEG)], axis=0))
            code_copy(f, d).start()
        for q in range(SEG):
            own[f, q] = row(c * SEG + q)

    def solve(f):
        total = own[f].reshape(SEG_ROWS, B)
        for d in PEERS:
            code_copy(f, d).wait_recv()
            total = total + decode(code_r[f, d, 0:SEG_ROWS], code_r[f, d, SEG_ROWS:CODED])
        return [
            lax.dot_general(
                rh[f, q] - total[q * P_SIZE : (q + 1) * P_SIZE], dv[f, q], NT,
                precision=lax.Precision.HIGHEST, preferred_element_type=jnp.float32,
            )
            for q in range(SEG)
        ]

    def to_cols(ref, ss, rr, size):
        mine = ref.at[pl.ds(c * size, size)]
        return [remote(mine, mine, ss.at[d], rr.at[d], (r, lax.rem(c + d, NZ))) for d in PEERS]

    def from_cols(ref, ss, rr, size, d):
        theirs = ref.at[pl.ds(lax.rem(c + NZ - d, NZ) * size, size)]
        remote(theirs, theirs, ss.at[d], rr.at[d], (r, c)).wait_recv()

    scatter(0, lambda s: product(0, s, known, old_index(0), (0, 1, 2)))

    even_col = lax.rem(c, 2) == 0

    def early(slots):
        def one(s, carry):
            part[s] = product(1, s, known, old_index(1), slots)
            return carry

        lax.fori_loop(0, ROWS_DEV, one, 0)

    pl.when(even_col)(lambda: early((1,)))
    pl.when(jnp.logical_not(even_col))(lambda: early((0, 2)))

    def asked(e, carry):
        remote(want, want_in.at[lax.rem(r + NR - e, NR)], w_s.at[e], w_r.at[e], (r, c)).wait_recv()
        return carry

    lax.fori_loop(1, NR, asked, 0)
    keep_own.wait()
    to_place.wait()
    to_scalar = pltpu.make_async_copy(want_in, sel, loc_sem.at[9])
    to_scalar.start()
    ld_dv.wait()
    ld_rh.wait()
    for q, value in enumerate(solve(0)):
        high = value.astype(jnp.bfloat16)
        low[c * SEG + q] = high
        rest[c * SEG + q] = (value - high.astype(jnp.float32)).astype(jnp.bfloat16)
    hi_out = to_cols(low, hi_s, hi_r, SEG)
    lo_out = to_cols(rest, lo_s, lo_r, SEG)
    for cp in hi_out:
        cp.start()
    to_scalar.wait()
    for d in PEERS:
        from_cols(low, hi_s, hi_r, SEG, d)

    def give(e, carry):
        peer = lax.rem(r + e, NR)
        a2a[e] = low[sel[peer, 0, r]]
        remote(a2a.at[e], recent.at[r], a_s.at[e], a_r.at[e], (peer, c)).start()
        return carry

    lax.fori_loop(1, NR, give, 0)
    recent[r] = low[sel[r, 0, r]]
    for cp in lo_out:
        cp.start()

    def take(e, carry):
        slot = recent.at[lax.rem(r + NR - e, NR)]
        remote(slot, slot, a_s.at[e], a_r.at[e], (r, c)).wait_recv()
        return carry

    lax.fori_loop(1, NR, take, 0)

    def late(slots):
        scatter(1, lambda s: part[s] + product(1, s, recent, new_index, slots))

    pl.when(even_col)(lambda: late((0, 2)))
    pl.when(jnp.logical_not(even_col))(lambda: late((1,)))

    for d in PEERS:
        from_cols(rest, lo_s, lo_r, SEG, d)
    out[0] = low[...].astype(jnp.float32) + rest[...].astype(jnp.float32)
    put(fin.at[c], jnp.concatenate(solve(1), axis=0))
    fin_out = to_cols(fin, fin_s, fin_r, 1)
    for cp in fin_out:
        cp.start()

    def show(z):
        value = decode(fin[z, 0:SEG_ROWS], fin[z, SEG_ROWS:CODED])
        out[1, pl.ds(z * SEG, SEG)] = value.reshape(SEG, P_SIZE, B)

    show(c)
    for cp in sends:
        cp.wait_send()
    for cp, h, item in sib:
        cp.wait_send()

    def left(e, carry):
        peer = lax.rem(r + e, NR)
        remote(want, want_in.at[r], w_s.at[e], w_r.at[e], (peer, c)).wait_send()
        remote(a2a.at[e], recent.at[r], a_s.at[e], a_r.at[e], (peer, c)).wait_send()
        return carry

    lax.fori_loop(1, NR, left, 0)
    for d in PEERS:
        code_copy(0, d).wait_send()
        code_copy(1, d).wait_send()
    for cp in hi_out + lo_out:
        cp.wait_send()
    for d in PEERS[::-1]:
        from_cols(fin, fin_s, fin_r, 1, d)
        show(lax.rem(c + NZ - d, NZ))
    for cp in fin_out:
        cp.wait_send()


def shards(owner_map, colidx, live, blocks, diag_inverse, right_side, prior):
    dma = pltpu.SemaphoreType.DMA
    hbm = pl.BlockSpec(memory_space=pltpu.HBM)
    operands = [owner_map, colidx.transpose(2, 0, 1), live, blocks, diag_inverse, right_side, prior]
    operands = [pltpu.with_memory_space_constraint(x, pltpu.HBM) for x in operands]
    return pl.pallas_call(
        kernel,
        out_shape=jax.ShapeDtypeStruct((2, ROWS_DEV, P_SIZE, B), jnp.float32),
        in_specs=[hbm] * 7,
        out_specs=pl.BlockSpec(memory_space=pltpu.VMEM),
        scratch_shapes=[
            pltpu.VMEM((NPRI + 1, P_SIZE, B), jnp.bfloat16),
            pltpu.VMEM((NR + 1, P_SIZE, B), jnp.bfloat16),
            pltpu.VMEM((2, ROWS_DEV, NBC, B, B), jnp.bfloat16),
            pltpu.VMEM((2, SEG, B, B), jnp.float32),
            pltpu.VMEM((2, SEG, P_SIZE, B), jnp.float32),
            pltpu.VMEM((ROWS_DEV, P_SIZE, B), jnp.float32),
            pltpu.VMEM((2, SEG, P_SIZE, B), jnp.float32),
            pltpu.VMEM((2, NZ, CODED, B), jnp.int16),
            pltpu.VMEM((2, NZ, CODED, B), jnp.int16),
            pltpu.VMEM((NZ, CODED, B), jnp.int16),
            pltpu.VMEM((ROWS_DEV, P_SIZE, B), jnp.bfloat16),
            pltpu.VMEM((ROWS_DEV, P_SIZE, B), jnp.bfloat16),
            pltpu.VMEM((NR, P_SIZE, B), jnp.bfloat16),
            pltpu.VMEM((2, ROWS_F), jnp.int32),
            pltpu.VMEM((SLOTS, 1, B), jnp.int32),
            pltpu.VMEM((1, B), jnp.int32),
            pltpu.VMEM((NR, 1, B), jnp.int32),
            pltpu.SMEM((NBC, 2, ROWS_DEV), jnp.int32),
            pltpu.SMEM((2, ROWS_DEV), jnp.int32),
            pltpu.SMEM((SLOTS, 1, B), jnp.int32),
            pltpu.SMEM((NR, 1, B), jnp.int32),
            dma((10,)),
            dma((NR,)), dma((NR,)),
            dma((36,)), dma((64,)),
            dma((32,)), dma((32,)),
            dma((2, NZ)), dma((2, NZ)),
            dma((NZ,)), dma((NZ,)),
            dma((NZ,)), dma((NZ,)),
            dma((NZ,)), dma((NZ,)),
            dma((NR,)), dma((NR,)),
        ],
        compiler_params=pltpu.CompilerParams(
            collective_id=0, has_side_effects=True, vmem_limit_bytes=48 * 1024 * 1024
        ),
    )(*operands)


def solution(mesh):
    placed = (
        P(),
        P(None, "rows", "cols"),
        P(None, "rows"),
        P(None, "rows", "cols", None, None),
        P(None, "rows", None, None),
        P(None, "rows", None, None),
        P("rows", None, None),
    )
    return jax.shard_map(
        shards, mesh=mesh, in_specs=placed, out_specs=P(None, "rows", None, None), check_vma=False
    )
```

time: 296 us -> 74.2 us (0.25); the launches traced: 292 us -> 74 us
  waiting for transfers between devices: 247 us -> 0 us
  Pallas kernels: 0 us -> 73 us
  local copies, waits for them, and re-layouts: 15.1 us -> 0.97 us
  matrix products: 13.7 us -> 0 us
  between operations: 13.3 us -> 0.01 us
    psum x2 -> x0, waiting for transfers between devices: 136 us -> none  [finish(): total = lax.psum(partial_value, 'cols')]
    all_gather x2 -> x0, waiting for transfers between devices: 110 us -> none  [the longest x1 56.1 us: shards(): prior_all = lax.all_gather(prior, 'rows', axis=0, tiled=True)]
    pallas_call x0 -> x1, Pallas kernels: none -> 73 us  [shards(): pl.pallas_call(kernel, out_shape=jax.ShapeDtypeStruct((2, ROWS_DEV, P_SIZ...]
    dot_general x4 -> x0, matrix products: 13.7 us -> none  [the longest x2 7.34 us: solve_diag(): jnp.einsum('rpb,rcb->rpc', resid, inverse, precision=lax.Precision.HIGHES...]
    gather x6 -> x0, local copies, waits for them, and re-layouts: 11.7 us -> none  [the longest x1 4.93 us: shards(): recent_values = whole_front[slot_pos]]
  transfers between devices with their start and end apart: 4 -> 0, of which waited for: 4 -> 0; matrix products, arithmetic and copies ran while one was open for 3% -> 0% of each run, Pallas kernels for 0% -> 0%
where the time goes in v2:
time: 74.2 us; the launch traced here: 74 us
  Pallas kernels  73 us (98%)
  local copies, waits for them, and re-layouts  0.97 us (1%)
    pallas_call x1, Pallas kernels, shards(): pl.pallas_call(kernel, out_shape=jax.ShapeDtypeStruct((2, ROWS_DEV, P_SIZ...  73 us

profile of v2, /device:TPU:1, one launch (start us, length us, event | category | flops | bytes accessed | tf_op | source)
XLA Modules:
  0.0 74.0 jit_solution(7449493175610288207)
XLA Ops:
  0.0 73.0 %shard_map.73 = f32[2,16,64,128]{3,2,1,0:T(8,128)S(1)} custom-call(s32[2,512]{1,0:T(2,128)} %owners.1, s32[3,2,16]{2,1,0:T(2,128)} %bitcast.1, s32[2,16]{1,0:T(2,128)} %live.1, bf16[2,16,3,128,128]{4,3,2,1,0:T(8,128)(2,1)} %blocks.1, f32[2,16,128,128]{3,2,1,0:T(8,128)} %dinv.1, f32[2,16,64,128]{3,2,1,0:T(8,128)} %rhs.1, bf16[8,64,128]{2,1,0:T(8,128)(2,1)} %prior.1), custom_call_target="tpu_custom_call" | custom-call | tf_op jit(solution)/shard_map/pallas_call | solution.py:356
  73.0 1.0 %copy.9 = f32[2,16,64,128]{3,2,1,0:T(8,128)} copy(f32[2,16,64,128]{3,2,1,0:T(8,128)S(1)} %shard_map.73) | data formatting | bytes 2097152

commit v3 on v2

--- a/solution.py
+++ b/solution.py
@@ -17,8 +17,8 @@
 NBC = 3
 SLOTS = ROWS_DEV * NBC
 P_SIZE, B = 64, 128
-SEG_ROWS = SEG * P_SIZE
-CODED = SEG_ROWS + 16
+POWER_ROWS = 16
+CODED = P_SIZE + POWER_ROWS
 NT = (((1,), (1,)), ((), ()))
 PEERS = (4, 3, 5, 2, 6, 1, 7)
 
@@ -27,14 +27,14 @@
     top = jnp.maximum(jnp.max(jnp.abs(value), axis=0, keepdims=True), 1e-30)
     power = jnp.ceil(jnp.log2(top) + 0.01)
     fixed = jnp.round(value * jnp.exp2(15.0 - power)).astype(jnp.int32).astype(jnp.int16)
-    powers = jnp.broadcast_to(power, (16, B)).astype(jnp.int32).astype(jnp.int16)
+    powers = jnp.broadcast_to(power, (POWER_ROWS, B)).astype(jnp.int32).astype(jnp.int16)
     return fixed, powers
 
 
 def decode(fixed, powers):
     unit = jnp.exp2(powers.astype(jnp.int32).astype(jnp.float32) - 15.0)
-    value = fixed.astype(jnp.int32).astype(jnp.float32).reshape(SEG_ROWS // 16, 16, B) * unit[None]
-    return value.reshape(SEG_ROWS, B)
+    value = fixed.astype(jnp.int32).astype(jnp.float32).reshape(P_SIZE // POWER_ROWS, POWER_ROWS, B) * unit[None]
+    return value.reshape(P_SIZE, B)
 
 
 def kernel(
@@ -151,18 +151,18 @@
     for h in (0, 1):
         push(h, (0, 0), (1, 0))
         push(h, (0, 0), (-1, 0))
+
+    def ask(e, carry):
+        peer = lax.rem(r + e, NR)
+        remote(want, want_in.at[r], w_s.at[e], w_r.at[e], (peer, c)).start()
+        return carry
+
+    lax.fori_loop(1, NR, ask, 0)
     for h in (0, 1):
         push(h, (0, 0), (2, 0))
         spread(h, (0, 0))
     for h in (0, 1):
         to_sibling(h, (0, 0))
-
-    def ask(e, carry):
-        peer = lax.rem(r + e, NR)
-        remote(want, want_in.at[r], w_s.at[e], w_r.at[e], (peer, c)).start()
-        return carry
-
-    lax.fori_loop(1, NR, ask, 0)
     keep_own = pltpu.make_async_copy(want, want_in.at[r], loc_sem.at[8])
     keep_own.start()
 
@@ -211,44 +211,45 @@
     def new_index(s, j):
         return jnp.where(c * NBC + j < live_s[1, s], place_s[s * NBC + j, 0, 0] >> 4, NR)
 
-    def code_copy(f, d):
+    part_rows = (pl.ds(0, CODED), pl.ds(CODED, P_SIZE))
+    row_at = (pl.ds(0, P_SIZE), pl.ds(CODED, P_SIZE))
+    power_at = pl.ds(P_SIZE, POWER_ROWS)
+
+    def code_copy(f, q, d):
         return remote(
-            code_s.at[f, d], code_r.at[f, d], rs_s.at[f, d], rs_r.at[f, d], (r, lax.rem(c + d, NZ))
+            code_s.at[f, d, part_rows[q]], code_r.at[f, d, part_rows[q]],
+            rs_s.at[f, q, d], rs_r.at[f, q, d], (r, lax.rem(c + d, NZ)),
         )
-
-    def put(ref, value):
-        fixed, powers = encode(value)
-        ref[0:SEG_ROWS] = fixed
-        ref[SEG_ROWS:CODED] = powers
 
     def scatter(f, row):
         for d in PEERS:
             peer = lax.rem(c + d, NZ)
-            put(code_s.at[f, d], jnp.concatenate([row(peer * SEG + q) for q in range(SEG)], axis=0))
-            code_copy(f, d).start()
+            fixed, powers = encode(jnp.concatenate([row(peer * SEG + q) for q in range(SEG)], axis=0))
+            code_s[f, d, row_at[0]] = fixed[:P_SIZE]
+            code_s[f, d, power_at] = powers
+            code_s[f, d, row_at[1]] = fixed[P_SIZE:]
+            code_copy(f, 0, d).start()
+        for d in PEERS:
+            code_copy(f, 1, d).start()
         for q in range(SEG):
             own[f, q] = row(c * SEG + q)
 
-    def solve(f):
-        total = own[f].reshape(SEG_ROWS, B)
+    def solve(f, q):
+        resid = rh[f, q] - own[f, q]
         for d in PEERS:
-            code_copy(f, d).wait_recv()
-            total = total + decode(code_r[f, d, 0:SEG_ROWS], code_r[f, d, SEG_ROWS:CODED])
-        return [
-            lax.dot_general(
-                rh[f, q] - total[q * P_SIZE : (q + 1) * P_SIZE], dv[f, q], NT,
-                precision=lax.Precision.HIGHEST, preferred_element_type=jnp.float32,
-            )
-            for q in range(SEG)
-        ]
-
-    def to_cols(ref, ss, rr, size):
-        mine = ref.at[pl.ds(c * size, size)]
-        return [remote(mine, mine, ss.at[d], rr.at[d], (r, lax.rem(c + d, NZ))) for d in PEERS]
-
-    def from_cols(ref, ss, rr, size, d):
-        theirs = ref.at[pl.ds(lax.rem(c + NZ - d, NZ) * size, size)]
-        remote(theirs, theirs, ss.at[d], rr.at[d], (r, c)).wait_recv()
+            code_copy(f, q, d).wait_recv()
+            resid = resid - decode(code_r[f, d, row_at[q]], code_r[f, d, power_at])
+        return lax.dot_general(
+            resid, dv[f, q], NT, precision=lax.Precision.HIGHEST, preferred_element_type=jnp.float32
+        )
+
+    def to_cols(ref, ss, rr, q):
+        mine = ref.at[c * SEG + q]
+        return [remote(mine, mine, ss.at[q, d], rr.at[q, d], (r, lax.rem(c + d, NZ))) for d in PEERS]
+
+    def from_cols(ref, ss, rr, q, d):
+        theirs = ref.at[lax.rem(c + NZ - d, NZ) * SEG + q]
+        remote(theirs, theirs, ss.at[q, d], rr.at[q, d], (r, c)).wait_recv()
 
     scatter(0, lambda s: product(0, s, known, old_index(0), (0, 1, 2)))
 
@@ -275,17 +276,21 @@
     to_scalar.start()
     ld_dv.wait()
     ld_rh.wait()
-    for q, value in enumerate(solve(0)):
+    hi_out, lo_out, fin_out = [], [], []
+    for q in range(SEG):
+        value = solve(0, q)
         high = value.astype(jnp.bfloat16)
         low[c * SEG + q] = high
         rest[c * SEG + q] = (value - high.astype(jnp.float32)).astype(jnp.bfloat16)
-    hi_out = to_cols(low, hi_s, hi_r, SEG)
-    lo_out = to_cols(rest, lo_s, lo_r, SEG)
-    for cp in hi_out:
-        cp.start()
+        new = to_cols(low, hi_s, hi_r, q)
+        for cp in new:
+            cp.start()
+        hi_out += new
+        lo_out += to_cols(rest, lo_s, lo_r, q)
     to_scalar.wait()
-    for d in PEERS:
-        from_cols(low, hi_s, hi_r, SEG, d)
+    for q in range(SEG):
+        for d in PEERS:
+            from_cols(low, hi_s, hi_r, q, d)
 
     def give(e, carry):
         peer = lax.rem(r + e, NR)
@@ -311,19 +316,24 @@
     pl.when(even_col)(lambda: late((0, 2)))
     pl.when(jnp.logical_not(even_col))(lambda: late((1,)))
 
-    for d in PEERS:
-        from_cols(rest, lo_s, lo_r, SEG, d)
+    for q in range(SEG):
+        for d in PEERS:
+            from_cols(rest, lo_s, lo_r, q, d)
     out[0] = low[...].astype(jnp.float32) + rest[...].astype(jnp.float32)
-    put(fin.at[c], jnp.concatenate(solve(1), axis=0))
-    fin_out = to_cols(fin, fin_s, fin_r, 1)
-    for cp in fin_out:
-        cp.start()
-
-    def show(z):
-        value = decode(fin[z, 0:SEG_ROWS], fin[z, SEG_ROWS:CODED])
-        out[1, pl.ds(z * SEG, SEG)] = value.reshape(SEG, P_SIZE, B)
-
-    show(c)
+
+    def show(row):
+        out[1, row] = decode(fin[row, row_at[0]], fin[row, power_at])
+
+    for q in range(SEG):
+        fixed, powers = encode(solve(1, q))
+        fin[c * SEG + q, row_at[0]] = fixed
+        fin[c * SEG + q, power_at] = powers
+        new = to_cols(fin, fin_s, fin_r, q)
+        for cp in new:
+            cp.start()
+        fin_out += new
+    for q in range(SEG):
+        show(c * SEG + q)
     for cp in sends:
         cp.wait_send()
     for cp, h, item in sib:
@@ -337,13 +347,15 @@
 
     lax.fori_loop(1, NR, left, 0)
     for d in PEERS:
-        code_copy(0, d).wait_send()
-        code_copy(1, d).wait_send()
+        for f in (0, 1):
+            for q in range(SEG):
+                code_copy(f, q, d).wait_send()
     for cp in hi_out + lo_out:
         cp.wait_send()
-    for d in PEERS[::-1]:
-        from_cols(fin, fin_s, fin_r, 1, d)
-        show(lax.rem(c + NZ - d, NZ))
+    for q in range(SEG):
+        for d in PEERS[::-1]:
+            from_cols(fin, fin_s, fin_r, q, d)
+            show(lax.rem(c + NZ - d, NZ) * SEG + q)
     for cp in fin_out:
         cp.wait_send()
 
@@ -366,9 +378,9 @@
             pltpu.VMEM((2, SEG, P_SIZE, B), jnp.float32),
             pltpu.VMEM((ROWS_DEV, P_SIZE, B), jnp.float32),
             pltpu.VMEM((2, SEG, P_SIZE, B), jnp.float32),
-            pltpu.VMEM((2, NZ, CODED, B), jnp.int16),
-            pltpu.VMEM((2, NZ, CODED, B), jnp.int16),
-            pltpu.VMEM((NZ, CODED, B), jnp.int16),
+            pltpu.VMEM((2, NZ, CODED + P_SIZE, B), jnp.int16),
+            pltpu.VMEM((2, NZ, CODED + P_SIZE, B), jnp.int16),
+            pltpu.VMEM((ROWS_DEV, CODED, B), jnp.int16),
             pltpu.VMEM((ROWS_DEV, P_SIZE, B), jnp.bfloat16),
             pltpu.VMEM((ROWS_DEV, P_SIZE, B), jnp.bfloat16),
             pltpu.VMEM((NR, P_SIZE, B), jnp.bfloat16),
@@ -384,10 +396,10 @@
             dma((NR,)), dma((NR,)),
             dma((36,)), dma((64,)),
             dma((32,)), dma((32,)),
-            dma((2, NZ)), dma((2, NZ)),
-            dma((NZ,)), dma((NZ,)),
-            dma((NZ,)), dma((NZ,)),
-            dma((NZ,)), dma((NZ,)),
+            dma((2, SEG, NZ)), dma((2, SEG, NZ)),
+            dma((SEG, NZ)), dma((SEG, NZ)),
+            dma((SEG, NZ)), dma((SEG, NZ)),
+            dma((SEG, NZ)), dma((SEG, NZ)),
             dma((NR,)), dma((NR,)),
         ],
         compiler_params=pltpu.CompilerParams(

time: 74.2 us -> 70.9 us (0.956)
  Pallas kernels: 73 us -> 69.9 us
    pallas_call x1, Pallas kernels: 73 us -> 69.9 us  [shards(): pl.pallas_call(kernel, out_shape=jax.ShapeDtypeStruct((2, ROWS_DEV, P_SIZ...]
where the time goes in v3:
time: 70.9 us
  Pallas kernels  69.9 us (99%)
  local copies, waits for them, and re-layouts  0.97 us (1%)
    pallas_call x1, Pallas kernels, shards(): pl.pallas_call(kernel, out_shape=jax.ShapeDtypeStruct((2, ROWS_DEV, P_SIZ...  69.9 us

profile of v3, /device:TPU:1, one launch (start us, length us, event | category | flops | bytes accessed | tf_op | source)
XLA Modules:
  0.0 70.9 jit_solution(6590219347815928304)
XLA Ops:
  0.0 69.9 %shard_map.73 = f32[2,16,64,128]{3,2,1,0:T(8,128)S(1)} custom-call(s32[2,512]{1,0:T(2,128)} %owners.1, s32[3,2,16]{2,1,0:T(2,128)} %bitcast.1, s32[2,16]{1,0:T(2,128)} %live.1, bf16[2,16,3,128,128]{4,3,2,1,0:T(8,128)(2,1)} %blocks.1, f32[2,16,128,128]{3,2,1,0:T(8,128)} %dinv.1, f32[2,16,64,128]{3,2,1,0:T(8,128)} %rhs.1, bf16[8,64,128]{2,1,0:T(8,128)(2,1)} %prior.1), custom_call_target="tpu_custom_call" | custom-call | tf_op jit(solution)/shard_map/pallas_call | solution.py:368
  69.9 1.0 %copy.9 = f32[2,16,64,128]{3,2,1,0:T(8,128)} copy(f32[2,16,64,128]{3,2,1,0:T(8,128)S(1)} %shard_map.73) | data formatting | bytes 2097152

commit v4 on v3

--- a/solution.py
+++ b/solution.py
@@ -17,10 +17,10 @@
 NBC = 3
 SLOTS = ROWS_DEV * NBC
 P_SIZE, B = 64, 128
-POWER_ROWS = 16
+POWER_ROWS = 8
 CODED = P_SIZE + POWER_ROWS
 NT = (((1,), (1,)), ((), ()))
-PEERS = (4, 3, 5, 2, 6, 1, 7)
+PEERS = (3, 5, 4, 2, 6, 1, 7)
 
 
 def encode(value):

time: 70.9 us -> 69.8 us (0.984)
  Pallas kernels: 69.9 us -> 68.5 us
    pallas_call x1, Pallas kernels: 69.9 us -> 68.5 us  [shards(): pl.pallas_call(kernel, out_shape=jax.ShapeDtypeStruct((2, ROWS_DEV, P_SIZ...]
where the time goes in v4:
time: 69.8 us; the launch traced here: 69.5 us
  Pallas kernels  68.5 us (98%)
  local copies, waits for them, and re-layouts  0.97 us (1%)
    pallas_call x1, Pallas kernels, shards(): pl.pallas_call(kernel, out_shape=jax.ShapeDtypeStruct((2, ROWS_DEV, P_SIZ...  68.5 us

profile of v4, /device:TPU:1, one launch (start us, length us, event | category | flops | bytes accessed | tf_op | source)
XLA Modules:
  0.0 69.5 jit_solution(14265728788857267158)
XLA Ops:
  0.0 68.5 %shard_map.73 = f32[2,16,64,128]{3,2,1,0:T(8,128)S(1)} custom-call(s32[2,512]{1,0:T(2,128)} %owners.1, s32[3,2,16]{2,1,0:T(2,128)} %bitcast.1, s32[2,16]{1,0:T(2,128)} %live.1, bf16[2,16,3,128,128]{4,3,2,1,0:T(8,128)(2,1)} %blocks.1, f32[2,16,128,128]{3,2,1,0:T(8,128)} %dinv.1, f32[2,16,64,128]{3,2,1,0:T(8,128)} %rhs.1, bf16[8,64,128]{2,1,0:T(8,128)(2,1)} %prior.1), custom_call_target="tpu_custom_call" | custom-call | tf_op jit(solution)/shard_map/pallas_call | solution.py:368
  68.5 1.0 %copy.9 = f32[2,16,64,128]{3,2,1,0:T(8,128)} copy(f32[2,16,64,128]{3,2,1,0:T(8,128)S(1)} %shard_map.73) | data formatting | bytes 2097152

commit v5 on v4

--- a/solution.py
+++ b/solution.py
@@ -21,6 +21,7 @@
 CODED = P_SIZE + POWER_ROWS
 NT = (((1,), (1,)), ((), ()))
 PEERS = (3, 5, 4, 2, 6, 1, 7)
+GATHER_PEERS = (4, 3, 5, 2, 6, 1, 7)
 
 
 def encode(value):
@@ -245,7 +246,7 @@
 
     def to_cols(ref, ss, rr, q):
         mine = ref.at[c * SEG + q]
-        return [remote(mine, mine, ss.at[q, d], rr.at[q, d], (r, lax.rem(c + d, NZ))) for d in PEERS]
+        return [remote(mine, mine, ss.at[q, d], rr.at[q, d], (r, lax.rem(c + d, NZ))) for d in GATHER_PEERS]
 
     def from_cols(ref, ss, rr, q, d):
         theirs = ref.at[lax.rem(c + NZ - d, NZ) * SEG + q]

time: 69.8 us -> 69.5 us (level)
  no operation moved by 1% of the time
where the time goes in v5:
time: 69.5 us; the launch traced here: 69.4 us
  Pallas kernels  68.4 us (98%)
  local copies, waits for them, and re-layouts  0.97 us (1%)
    pallas_call x1, Pallas kernels, shards(): pl.pallas_call(kernel, out_shape=jax.ShapeDtypeStruct((2, ROWS_DEV, P_SIZ...  68.4 us

profile of v5, /device:TPU:1, one launch (start us, length us, event | category | flops | bytes accessed | tf_op | source)
XLA Modules:
  0.0 69.4 jit_solution(2575370261797859617)
XLA Ops:
  0.0 68.4 %shard_map.73 = f32[2,16,64,128]{3,2,1,0:T(8,128)S(1)} custom-call(s32[2,512]{1,0:T(2,128)} %owners.1, s32[3,2,16]{2,1,0:T(2,128)} %bitcast.1, s32[2,16]{1,0:T(2,128)} %live.1, bf16[2,16,3,128,128]{4,3,2,1,0:T(8,128)(2,1)} %blocks.1, f32[2,16,128,128]{3,2,1,0:T(8,128)} %dinv.1, f32[2,16,64,128]{3,2,1,0:T(8,128)} %rhs.1, bf16[8,64,128]{2,1,0:T(8,128)(2,1)} %prior.1), custom_call_target="tpu_custom_call" | custom-call | tf_op jit(solution)/shard_map/pallas_call | solution.py:369
  68.4 1.0 %copy.9 = f32[2,16,64,128]{3,2,1,0:T(8,128)} copy(f32[2,16,64,128]{3,2,1,0:T(8,128)S(1)} %shard_map.73) | data formatting | bytes 2097152
